TPU v7x, 256 devices: a whole 4x4x8 slice. The times are simulated.
256 devices in a mesh: row: 16 (over y, z_lo, core), col: 16 (over z_hi, x).
Axes of the slice: x: 4, y: 4, z: 8 (z_hi: 4, z_lo: 2; z = z_hi * 2 + z_lo), core: 2. Of those that a mesh axis runs over, the one named last changes fastest.
Arguments:
- features: bfloat16 [131072, 256], P(('row', 'col')), may hold values from -6 to 6
- w_self: bfloat16 [256, 256], replicated, may hold values from -0.375 to 0.375
- w_neigh: bfloat16 [256, 256], replicated, may hold values from -3 to 3
- cotangent: bfloat16 [131072, 256], P(('row', 'col')), may hold values from -6 to 6
- degree: int32 [131072], P(('row', 'col')), may hold values from 64 to 256
- tile_rows: int32 [65536], P(('row', 'col')), may hold values from 0 to 63
- tile_cols: int32 [65536], P(('row', 'col')), may hold values from 0 to 63
- tile_edges: int32 [4, 65536, 128], P(None, ('row', 'col')), may hold values from 0 to 127
- tile_count: int32 [256], P(('row', 'col')), may hold values from 4 to 256, as said below
Outputs:
- activations: bfloat16 [131072, 256], P(('row', 'col'))
- feature_grad: bfloat16 [131072, 256], P(('row', 'col'))
- grad_self: float32 [256, 256], replicated
- grad_neigh: float32 [256, 256], replicated
Inputs may be any that keep to these rules, and one draw needn't show every extreme that they name: The busiest device uses all 256 of its slots; slots from tile_count on are ignored.
All inputs are finite; a program needn't handle non-finite values.
Results may differ from a plain program's by a relative error of at most 0.0059.
Values may be sent and summed in bfloat16 or wider, within the bound.
No kernel may reach another device: no remote copies, remote signals or barrier semaphores. Data moves between devices by JAX's collectives and lax.ppermute only.
A program may use at most 64 MiB of HBM per device.

v0:
```python
import math
import jax
import jax.numpy as jnp
from jax import lax
from jax.sharding import PartitionSpec as P


def tile_masks(edges_here, use_here):
    tile_size = edges_here.shape[2]
    matches = edges_here[:, :, :, None] == jnp.arange(tile_size, dtype=jnp.int32)
    multiplicity = jnp.sum(matches.astype(jnp.float32), axis=0)
    return (multiplicity * use_here[:, None, None]).astype(jnp.bfloat16)


def sum_weights(part_self, part_neigh):
    return lax.psum((part_self, part_neigh), ("row", "col"))


def spread_back(dscaled, row_blocks, col_blocks, edge_blocks, use_blocks, col_tile_count):
    tile_size = edge_blocks.shape[3]
    feature_dim = dscaled.shape[1]
    row_nodes = lax.all_gather(dscaled, "col", axis=0, tiled=True)
    row_tiles = row_nodes.reshape(-1, tile_size, feature_dim)

    def backward_round(running, inputs):
        rows_here, cols_here, edges_here, use_here = inputs
        pattern = tile_masks(edges_here, use_here)
        contribution = jnp.einsum(
            "bqc,bqf->bcf", pattern, row_tiles[rows_here], preferred_element_type=jnp.float32
        )
        return (running.at[cols_here].add(contribution), None)

    start_value = jnp.zeros((col_tile_count, tile_size, feature_dim), jnp.float32)
    partial_grads, _ = lax.scan(
        backward_round, start_value, (row_blocks, col_blocks, edge_blocks, use_blocks)
    )
    return lax.psum_scatter(
        partial_grads.reshape(-1, feature_dim), "row", scatter_dimension=0, tiled=True
    )


def per_device(
    features, w_self, w_neigh, cotangent, degree, tile_rows, tile_cols, tile_edges, tile_count
):
    local_rows, feature_dim = features.shape
    tile_size = tile_edges.shape[2]
    slot_count = tile_rows.shape[0]
    row_devices = lax.axis_size("row")
    col_devices = lax.axis_size("col")
    in_use = (jnp.arange(slot_count, dtype=jnp.int32) < tile_count[0]).astype(jnp.float32)
    block_size = math.gcd(slot_count, 32)
    rounds = slot_count // block_size
    edge_blocks = tile_edges.reshape(tile_edges.shape[0], rounds, block_size, tile_size).transpose(
        1, 0, 2, 3
    )
    row_blocks = tile_rows.reshape(rounds, block_size)
    col_blocks = tile_cols.reshape(rounds, block_size)
    use_blocks = in_use.reshape(rounds, block_size)
    row_tile_count = local_rows * col_devices // tile_size
    col_tile_count = local_rows * row_devices // tile_size
    column_nodes = lax.all_gather(features, "row", axis=0, tiled=True)
    column_tiles = column_nodes.reshape(-1, tile_size, feature_dim)

    def forward_round(running, inputs):
        rows_here, cols_here, edges_here, use_here = inputs
        pattern = tile_masks(edges_here, use_here)
        product = jnp.einsum(
            "bqc,bcf->bqf", pattern, column_tiles[cols_here], preferred_element_type=jnp.float32
        )
        return (running.at[rows_here].add(product), None)

    start_value = jnp.zeros((row_tile_count, tile_size, feature_dim), jnp.float32)
    partial_sums, _ = lax.scan(
        forward_round, start_value, (row_blocks, col_blocks, edge_blocks, use_blocks)
    )
    neighbour_sum = lax.psum_scatter(
        partial_sums.reshape(-1, feature_dim), "col", scatter_dimension=0, tiled=True
    )
    degree_wide = degree.astype(jnp.float32)[:, None]
    aggregate = (neighbour_sum / degree_wide).astype(jnp.bfloat16)
    preact = jnp.dot(features, w_self, preferred_element_type=jnp.float32) + jnp.dot(
        aggregate, w_neigh, preferred_element_type=jnp.float32
    )
    sigmoid_pre = jax.nn.sigmoid(preact)
    activations = (preact * sigmoid_pre).astype(jnp.bfloat16)
    slope = sigmoid_pre * (1.0 + preact * (1.0 - sigmoid_pre))
    dpreact = (cotangent.astype(jnp.float32) * slope).astype(jnp.bfloat16)
    part_self = jnp.einsum("nf,ng->fg", features, dpreact, preferred_element_type=jnp.float32)
    part_neigh = jnp.einsum("nf,ng->fg", aggregate, dpreact, preferred_element_type=jnp.float32)
    dscaled = (
        jnp.einsum("ng,fg->nf", dpreact, w_neigh, preferred_element_type=jnp.float32) / degree_wide
    ).astype(jnp.bfloat16)
    neighbour_grad = spread_back(
        dscaled, row_blocks, col_blocks, edge_blocks, use_blocks, col_tile_count
    )
    grad_pair = sum_weights(part_self, part_neigh)
    own_grad = jnp.einsum("ng,fg->nf", dpreact, w_self, preferred_element_type=jnp.float32)
    feature_grad = (own_grad + neighbour_grad).astype(jnp.bfloat16)
    total_nodes = local_rows * row_devices * col_devices
    grad_scale = 1.0 / math.sqrt(total_nodes)
    return (activations, feature_grad, grad_pair[0] * grad_scale, grad_pair[1] * grad_scale)


def solution(mesh):
    return jax.shard_map(
        per_device,
        mesh=mesh,
        in_specs=(
            P(("row", "col"), None),
            P(),
            P(),
            P(("row", "col"), None),
            P(("row", "col")),
            P(("row", "col")),
            P(("row", "col")),
            P(None, ("row", "col"), None),
            P(("row", "col")),
        ),
        out_specs=(P(("row", "col"), None), P(("row", "col"), None), P(), P()),
        check_vma=False,
    )
```

profile of v0, /device:TPU:2, one launch (start us, length us, event | category | flops | bytes accessed | tf_op | source)
XLA Modules:
  0.0 771.7 jit_solution(11886097251280555593)
XLA Ops:
  11.2 41.7 %all-gather.3.cloned.1.call-done = bf16[8192,256]{1,0:T(8,128)(2,1)} async-done(((bf16[512,256]{1,0:T(8,128)(2,1)}), bf16[8192,256]{1,0:T(8,128)(2,1)}) %all-gather.3.cloned.1.call-update) | async-done | bytes 4194320 | tf_op jit(solution)/shard_map/all_gather | solution.py:61
  52.9 4.3 broadcast.81.clone
  57.1 147.1 %while.20 = (s32[]{:T(128)}, f32[64,128,256]{2,1,0:T(8,128)}, s32[8,32]{1,0:T(8,128)S(1)}, s32[8,4,32,128]{3,2,1,0:T(8,128)S(1)}, f32[8,32]{1,0:T(8,128)S(1)}, /...) while((s32[]{:T(128)}, f32[64,128,256]{2,1,0:T(8,128)}, s32[8,32]{1,0:T(8,128)S(1)}, ...), condition=%wide.region_3.4_spmd, body=%wide.region_0.3_spmd.sunk | while | flops 276300992 | bytes 27465064 | solution.py:73
  60.1 2.9 convert_reduce_fusion.4
  65.7 9.8 %scatter_fusion = f32[64,128,256]{2,1,0:T(8,128)} fusion(f32[64,128,256]{2,1,0:T(8,128)} %get-tuple-element.261, s32[32]{0:T(128)S(1)} %get-tuple-element.241, f32[32,128,256]{2,1,0:T(8,128)} %fusion.44), kind=kCustom, calls=%fused_computation.2.clone.1 | custom fusion | flops 1048576 | bytes 12583040 | tf_op jit(solution)/shard_map/while/body/eval_jaxpr/scatter-add | solution.py:70
  78.5 2.9 convert_reduce_fusion.4
  84.2 9.7 %scatter_fusion = f32[64,128,256]{2,1,0:T(8,128)} fusion(f32[64,128,256]{2,1,0:T(8,128)} %get-tuple-element.261, s32[32]{0:T(128)S(1)} %get-tuple-element.241, f32[32,128,256]{2,1,0:T(8,128)} %fusion.44), kind=kCustom, calls=%fused_computation.2.clone.1 | custom fusion | flops 1048576 | bytes 12583040 | tf_op jit(solution)/shard_map/while/body/eval_jaxpr/scatter-add | solution.py:70
  96.7 2.9 convert_reduce_fusion.4
  102.4 9.7 %scatter_fusion = f32[64,128,256]{2,1,0:T(8,128)} fusion(f32[64,128,256]{2,1,0:T(8,128)} %get-tuple-element.261, s32[32]{0:T(128)S(1)} %get-tuple-element.241, f32[32,128,256]{2,1,0:T(8,128)} %fusion.44), kind=kCustom, calls=%fused_computation.2.clone.1 | custom fusion | flops 1048576 | bytes 12583040 | tf_op jit(solution)/shard_map/while/body/eval_jaxpr/scatter-add | solution.py:70
  115.0 2.9 convert_reduce_fusion.4
  120.7 9.6 %scatter_fusion = f32[64,128,256]{2,1,0:T(8,128)} fusion(f32[64,128,256]{2,1,0:T(8,128)} %get-tuple-element.261, s32[32]{0:T(128)S(1)} %get-tuple-element.241, f32[32,128,256]{2,1,0:T(8,128)} %fusion.44), kind=kCustom, calls=%fused_computation.2.clone.1 | custom fusion | flops 1048576 | bytes 12583040 | tf_op jit(solution)/shard_map/while/body/eval_jaxpr/scatter-add | solution.py:70
  133.3 2.9 convert_reduce_fusion.4
  139.0 9.8 %scatter_fusion = f32[64,128,256]{2,1,0:T(8,128)} fusion(f32[64,128,256]{2,1,0:T(8,128)} %get-tuple-element.261, s32[32]{0:T(128)S(1)} %get-tuple-element.241, f32[32,128,256]{2,1,0:T(8,128)} %fusion.44), kind=kCustom, calls=%fused_computation.2.clone.1 | custom fusion | flops 1048576 | bytes 12583040 | tf_op jit(solution)/shard_map/while/body/eval_jaxpr/scatter-add | solution.py:70
  151.6 2.9 convert_reduce_fusion.4
  157.3 9.8 %scatter_fusion = f32[64,128,256]{2,1,0:T(8,128)} fusion(f32[64,128,256]{2,1,0:T(8,128)} %get-tuple-element.261, s32[32]{0:T(128)S(1)} %get-tuple-element.241, f32[32,128,256]{2,1,0:T(8,128)} %fusion.44), kind=kCustom, calls=%fused_computation.2.clone.1 | custom fusion | flops 1048576 | bytes 12583040 | tf_op jit(solution)/shard_map/while/body/eval_jaxpr/scatter-add | solution.py:70
  170.0 2.9 convert_reduce_fusion.4
  175.7 9.9 %scatter_fusion = f32[64,128,256]{2,1,0:T(8,128)} fusion(f32[64,128,256]{2,1,0:T(8,128)} %get-tuple-element.261, s32[32]{0:T(128)S(1)} %get-tuple-element.241, f32[32,128,256]{2,1,0:T(8,128)} %fusion.44), kind=kCustom, calls=%fused_computation.2.clone.1 | custom fusion | flops 1048576 | bytes 12583040 | tf_op jit(solution)/shard_map/while/body/eval_jaxpr/scatter-add | solution.py:70
  188.5 2.9 convert_reduce_fusion.4
  194.2 10.0 %scatter_fusion = f32[64,128,256]{2,1,0:T(8,128)} fusion(f32[64,128,256]{2,1,0:T(8,128)} %get-tuple-element.261, s32[32]{0:T(128)S(1)} %get-tuple-element.241, f32[32,128,256]{2,1,0:T(8,128)} %fusion.44), kind=kCustom, calls=%fused_computation.2.clone.1 | custom fusion | flops 1048576 | bytes 12583040 | tf_op jit(solution)/shard_map/while/body/eval_jaxpr/scatter-add | solution.py:70
  205.4 119.9 %reduce-scatter.3.cloned.1.call-done = f32[512,256]{1,0:T(8,128)} async-done(((f32[8192,256]{1,0:T(8,128)}), f32[512,256]{1,0:T(8,128)}) %reduce-scatter.3.cloned.1.call-update) | async-done | bytes 524304 | tf_op jit(solution)/shard_map/reduce_scatter | solution.py:76
  330.7 72.7 %all-gather.5.cloned.1.call-done = bf16[8192,256]{1,0:T(8,128)(2,1)} async-done(((bf16[512,256]{1,0:T(8,128)(2,1)}), bf16[8192,256]{1,0:T(8,128)(2,1)}) %all-gather.5.cloned.1.call-update) | async-done | bytes 4194320 | tf_op jit(solution)/shard_map/all_gather | solution.py:22
  403.4 4.3 broadcast.81
  407.6 150.2 %while.21 = (s32[]{:T(128)}, f32[64,128,256]{2,1,0:T(8,128)}, s32[8,32]{1,0:T(8,128)S(1)}, s32[8,4,32,128]{3,2,1,0:T(8,128)S(1)}, f32[8,32]{1,0:T(8,128)S(1)}, /...) while((s32[]{:T(128)}, f32[64,128,256]{2,1,0:T(8,128)}, s32[8,32]{1,0:T(8,128)S(1)}, ...), condition=%wide.region_8.9_spmd, body=%wide.region_5.8_spmd.sunk | while | flops 276300992 | bytes 27465064 | solution.py:34
  410.5 2.9 convert_reduce_fusion.5
  416.4 9.9 %scatter_fusion.1 = f32[64,128,256]{2,1,0:T(8,128)} fusion(f32[64,128,256]{2,1,0:T(8,128)} %get-tuple-element.285, s32[32]{0:T(128)S(1)} %get-tuple-element.250, f32[32,128,256]{2,1,0:T(8,128)} %fusion.48), kind=kCustom, calls=%fused_computation.3.clone.1 | custom fusion | flops 1048576 | bytes 12583040 | tf_op jit(solution)/shard_map/while/body/eval_jaxpr/scatter-add | solution.py:31
  429.2 2.9 convert_reduce_fusion.5
  432.2 2.9 fusion.48
  435.1 10.1 %scatter_fusion.1 = f32[64,128,256]{2,1,0:T(8,128)} fusion(f32[64,128,256]{2,1,0:T(8,128)} %get-tuple-element.285, s32[32]{0:T(128)S(1)} %get-tuple-element.250, f32[32,128,256]{2,1,0:T(8,128)} %fusion.48), kind=kCustom, calls=%fused_computation.3.clone.1 | custom fusion | flops 1048576 | bytes 12583040 | tf_op jit(solution)/shard_map/while/body/eval_jaxpr/scatter-add | solution.py:31
  445.2 2.9 gather_fusion.1
  448.1 2.9 convert_reduce_fusion.5
  451.0 2.9 fusion.48
  453.9 10.0 %scatter_fusion.1 = f32[64,128,256]{2,1,0:T(8,128)} fusion(f32[64,128,256]{2,1,0:T(8,128)} %get-tuple-element.285, s32[32]{0:T(128)S(1)} %get-tuple-element.250, f32[32,128,256]{2,1,0:T(8,128)} %fusion.48), kind=kCustom, calls=%fused_computation.3.clone.1 | custom fusion | flops 1048576 | bytes 12583040 | tf_op jit(solution)/shard_map/while/body/eval_jaxpr/scatter-add | solution.py:31
  466.9 2.9 convert_reduce_fusion.5
  469.8 2.9 fusion.48
  472.7 10.0 %scatter_fusion.1 = f32[64,128,256]{2,1,0:T(8,128)} fusion(f32[64,128,256]{2,1,0:T(8,128)} %get-tuple-element.285, s32[32]{0:T(128)S(1)} %get-tuple-element.250, f32[32,128,256]{2,1,0:T(8,128)} %fusion.48), kind=kCustom, calls=%fused_computation.3.clone.1 | custom fusion | flops 1048576 | bytes 12583040 | tf_op jit(solution)/shard_map/while/body/eval_jaxpr/scatter-add | solution.py:31
  485.7 2.9 convert_reduce_fusion.5
  491.5 10.1 %scatter_fusion.1 = f32[64,128,256]{2,1,0:T(8,128)} fusion(f32[64,128,256]{2,1,0:T(8,128)} %get-tuple-element.285, s32[32]{0:T(128)S(1)} %get-tuple-element.250, f32[32,128,256]{2,1,0:T(8,128)} %fusion.48), kind=kCustom, calls=%fused_computation.3.clone.1 | custom fusion | flops 1048576 | bytes 12583040 | tf_op jit(solution)/shard_map/while/body/eval_jaxpr/scatter-add | solution.py:31
  501.6 2.9 gather_fusion.1
  504.5 2.9 convert_reduce_fusion.5
  510.4 10.1 %scatter_fusion.1 = f32[64,128,256]{2,1,0:T(8,128)} fusion(f32[64,128,256]{2,1,0:T(8,128)} %get-tuple-element.285, s32[32]{0:T(128)S(1)} %get-tuple-element.250, f32[32,128,256]{2,1,0:T(8,128)} %fusion.48), kind=kCustom, calls=%fused_computation.3.clone.1 | custom fusion | flops 1048576 | bytes 12583040 | tf_op jit(solution)/shard_map/while/body/eval_jaxpr/scatter-add | solution.py:31
  523.4 2.9 convert_reduce_fusion.5
  526.3 2.9 fusion.48
  529.2 9.9 %scatter_fusion.1 = f32[64,128,256]{2,1,0:T(8,128)} fusion(f32[64,128,256]{2,1,0:T(8,128)} %get-tuple-element.285, s32[32]{0:T(128)S(1)} %get-tuple-element.250, f32[32,128,256]{2,1,0:T(8,128)} %fusion.48), kind=kCustom, calls=%fused_computation.3.clone.1 | custom fusion | flops 1048576 | bytes 12583040 | tf_op jit(solution)/shard_map/while/body/eval_jaxpr/scatter-add | solution.py:31
  542.1 2.9 convert_reduce_fusion.5
  545.0 2.9 fusion.48
  547.9 10.0 %scatter_fusion.1 = f32[64,128,256]{2,1,0:T(8,128)} fusion(f32[64,128,256]{2,1,0:T(8,128)} %get-tuple-element.285, s32[32]{0:T(128)S(1)} %get-tuple-element.250, f32[32,128,256]{2,1,0:T(8,128)} %fusion.48), kind=kCustom, calls=%fused_computation.3.clone.1 | custom fusion | flops 1048576 | bytes 12583040 | tf_op jit(solution)/shard_map/while/body/eval_jaxpr/scatter-add | solution.py:31
  557.9 103.7 %all-reduce.3.cloned.1.call-done = (f32[256,256]{0,1:T(8,128)}, f32[256,256]{0,1:T(8,128)}) async-done(((f32[256,256]{0,1:T(8,128)}, f32[256,256]{0,1:T(8,128)}), (f32[256,256]{0,1:T(8,128)}, f32[256,256]{0,1:T(8,128)})) %all-reduce.3.cloned.1.call-update) | async-done | bytes 524304 | tf_op jit(solution)/shard_map/psum | solution.py:16
  664.4 98.7 %reduce-scatter.5.cloned.1.call-done = f32[512,256]{1,0:T(8,128)} async-done(((f32[8192,256]{1,0:T(8,128)}), f32[512,256]{1,0:T(8,128)}) %reduce-scatter.5.cloned.1.call-update) | async-done | bytes 524304 | tf_op jit(solution)/shard_map/reduce_scatter | solution.py:37
  (124 shorter events, 85.9 us)
Async XLA Ops:
  7.2 319.3 %copy-start = (bf16[256,256]{1,0:T(8,128)(2,1)S(1)}, bf16[256,256]{1,0:T(8,128)(2,1)}, u32[]{:S(2)}) copy-start(bf16[256,256]{1,0:T(8,128)(2,1)} %param.15) | copy-start | bytes 393220
  7.2 45.7 %all-gather.3.cloned.1.call-start = ((), (), s32[]{:S(2)}) async-start(), calls=%async_computation.2 | async-start | bytes 4456448 | tf_op jit(solution)/shard_map/all_gather | solution.py:61
  7.9 317.4 %reduce-scatter.3.cloned.1.call-start = ((), (), s32[]{:S(2)}) async-start(), calls=%async_computation.3 | async-start | bytes 8912896 | tf_op jit(solution)/shard_map/reduce_scatter | solution.py:76
  204.2 0.7 copy-start.3
  204.2 1.0 copy-start.1
  204.2 1.0 copy-start.2
  204.2 122.3 %copy-start.4 = (bf16[512,256]{1,0:T(8,128)(2,1)S(1)}, bf16[512,256]{1,0:T(8,128)(2,1)}, u32[]{:S(2)}) copy-start(bf16[512,256]{1,0:T(8,128)(2,1)} %param.16) | copy-start | bytes 786436
  204.2 199.1 %all-gather.5.cloned.1.call-start = ((), (), s32[]{:S(2)}) async-start(), calls=%async_computation.4 | async-start | bytes 4456448 | tf_op jit(solution)/shard_map/all_gather | solution.py:22
  328.6 333.0 %all-reduce.3.cloned.1.call-start = ((), (), s32[]{:S(2)}) async-start(), calls=%async_computation.6 | async-start | bytes 1048576 | tf_op jit(solution)/shard_map/psum | solution.py:16
  330.6 432.5 %reduce-scatter.5.cloned.1.call-start = ((), (), s32[]{:S(2)}) async-start(), calls=%async_computation.5 | async-start | bytes 8912896 | tf_op jit(solution)/shard_map/reduce_scatter | solution.py:37
Sparse Core Ops, SparseCore 0:
  9.9 42.9 all-gather.2
  204.4 120.8 reduce-scatter.2
  328.7 74.6 all-gather.4
  409.4 252.1 all-reduce.2
  664.0 99.0 reduce-scatter.4
where the time goes:
time: 773 us; the launch traced here: 772 us
  waiting for transfers between devices  437 us (57%)
  other arithmetic  208 us (27%)
  local copies, waits for them, and re-layouts  60 us (8%)
  matrix products  51.1 us (7%)
  between operations  14.5 us (2%)
    reduce_scatter x1, waiting for transfers between devices, per_device(): lax.psum_scatter(partial_sums.reshape(-1, feature_dim), 'col', scatter_di...  120 us
    psum x1, waiting for transfers between devices, sum_weights(): return lax.psum((part_self, part_neigh), ('row', 'col'))  104 us
    reduce_scatter x1, waiting for transfers between devices, spread_back(): lax.psum_scatter(partial_grads.reshape(-1, feature_dim), 'row', scatter_d...  98.7 us
    scatter-add x8, other arithmetic, backward_round(): return (running.at[cols_here].add(contribution), None)  80.1 us
    scatter-add x8, other arithmetic, forward_round(): return (running.at[rows_here].add(product), None)  78.3 us
    all_gather x1, waiting for transfers between devices, spread_back(): row_nodes = lax.all_gather(dscaled, 'col', axis=0, tiled=True)  72.7 us
    reduce_sum x16, other arithmetic, tile_masks(): multiplicity = jnp.sum(matches.astype(jnp.float32), axis=0)  46.9 us
    all_gather x1, waiting for transfers between devices, per_device(): column_nodes = lax.all_gather(features, 'row', axis=0, tiled=True)  41.7 us
  transfers between devices with their start and end apart: 5, of which 5 were waited for; matrix products, arithmetic and copies ran while one was open for 21% of the time, Pallas kernels for 0%

commit v1 on v0

--- a/solution.py
+++ b/solution.py
@@ -13,7 +13,13 @@
 
 
 def sum_weights(part_self, part_neigh):
-    return lax.psum((part_self, part_neigh), ("row", "col"))
+
+    def trails_take(load, chip_axis, link_axis):
+        z = jax.lax.psum(load, axis_name=chip_axis)
+        vec_out = jax.lax.psum(z, link_axis)
+        return vec_out
+
+    return trails_take((part_self, part_neigh), "row", "col")
 
 
 def spread_back(dscaled, row_blocks, col_blocks, edge_blocks, use_blocks, col_tile_count):

time: 773 us -> 810 us (1.048)
  waiting for transfers between devices: 437 us -> 475 us
    psum x1 -> x2, waiting for transfers between devices: 104 us -> 134 us  [the longest x1 120 us: trails_take(): z = jax.lax.psum(load, axis_name=chip_axis)]
  transfers between devices with their start and end apart: 5 -> 6, of which waited for: 5 -> 6; matrix products, arithmetic and copies ran while one was open for 21% -> 20% of each run, Pallas kernels for 0% -> 0%
where the time goes in v1:
time: 810 us; the launch traced here: 809 us
  waiting for transfers between devices  475 us (59%)
  other arithmetic  208 us (26%)
  local copies, waits for them, and re-layouts  60 us (7%)
  matrix products  51 us (6%)
  between operations  14.8 us (2%)
    psum x1, waiting for transfers between devices, trails_take(): z = jax.lax.psum(load, axis_name=chip_axis)  120 us
    reduce_scatter x1, waiting for transfers between devices, per_device(): lax.psum_scatter(partial_sums.reshape(-1, feature_dim), 'col', scatter_di...  120 us
    reduce_scatter x1, waiting for transfers between devices, spread_back(): lax.psum_scatter(partial_grads.reshape(-1, feature_dim), 'row', scatter_d...  99 us
    scatter-add x8, other arithmetic, backward_round(): return (running.at[cols_here].add(contribution), None)  80.1 us
    all_gather x1, waiting for transfers between devices, spread_back(): row_nodes = lax.all_gather(dscaled, 'col', axis=0, tiled=True)  79.2 us
    scatter-add x8, other arithmetic, forward_round(): return (running.at[rows_here].add(product), None)  78.2 us
    reduce_sum x16, other arithmetic, tile_masks(): multiplicity = jnp.sum(matches.astype(jnp.float32), axis=0)  46.9 us
    all_gather x1, waiting for transfers between devices, per_device(): column_nodes = lax.all_gather(features, 'row', axis=0, tiled=True)  41.7 us
  transfers between devices with their start and end apart: 6, of which 6 were waited for; matrix products, arithmetic and copies ran while one was open for 20% of the time, Pallas kernels for 0%

profile of v1, /device:TPU:2, one launch (start us, length us, event | category | flops | bytes accessed | tf_op | source)
XLA Modules:
  0.0 809.0 jit_solution(18381005559218769921)
XLA Ops:
  11.2 41.7 %all-gather.3.cloned.1.call-done = bf16[8192,256]{1,0:T(8,128)(2,1)} async-done(((bf16[512,256]{1,0:T(8,128)(2,1)}), bf16[8192,256]{1,0:T(8,128)(2,1)}) %all-gather.3.cloned.1.call-update) | async-done | bytes 4194320 | tf_op jit(solution)/shard_map/all_gather | solution.py:67
  52.9 4.3 broadcast.81.clone
  57.1 146.8 %while.20 = (s32[]{:T(128)}, f32[64,128,256]{2,1,0:T(8,128)}, s32[8,32]{1,0:T(8,128)S(1)}, s32[8,4,32,128]{3,2,1,0:T(8,128)S(1)}, f32[8,32]{1,0:T(8,128)S(1)}, /...) while((s32[]{:T(128)}, f32[64,128,256]{2,1,0:T(8,128)}, s32[8,32]{1,0:T(8,128)S(1)}, ...), condition=%wide.region_3.4_spmd, body=%wide.region_0.3_spmd.sunk | while | flops 276300992 | bytes 27465064 | solution.py:79
  60.1 2.9 convert_reduce_fusion.4
  65.7 9.8 %scatter_fusion = f32[64,128,256]{2,1,0:T(8,128)} fusion(f32[64,128,256]{2,1,0:T(8,128)} %get-tuple-element.263, s32[32]{0:T(128)S(1)} %get-tuple-element.243, f32[32,128,256]{2,1,0:T(8,128)} %fusion.44), kind=kCustom, calls=%fused_computation.2.clone.1 | custom fusion | flops 1048576 | bytes 12583040 | tf_op jit(solution)/shard_map/while/body/eval_jaxpr/scatter-add | solution.py:76
  78.5 2.9 convert_reduce_fusion.4
  84.1 9.7 %scatter_fusion = f32[64,128,256]{2,1,0:T(8,128)} fusion(f32[64,128,256]{2,1,0:T(8,128)} %get-tuple-element.263, s32[32]{0:T(128)S(1)} %get-tuple-element.243, f32[32,128,256]{2,1,0:T(8,128)} %fusion.44), kind=kCustom, calls=%fused_computation.2.clone.1 | custom fusion | flops 1048576 | bytes 12583040 | tf_op jit(solution)/shard_map/while/body/eval_jaxpr/scatter-add | solution.py:76
  96.7 2.9 convert_reduce_fusion.4
  102.4 9.7 %scatter_fusion = f32[64,128,256]{2,1,0:T(8,128)} fusion(f32[64,128,256]{2,1,0:T(8,128)} %get-tuple-element.263, s32[32]{0:T(128)S(1)} %get-tuple-element.243, f32[32,128,256]{2,1,0:T(8,128)} %fusion.44), kind=kCustom, calls=%fused_computation.2.clone.1 | custom fusion | flops 1048576 | bytes 12583040 | tf_op jit(solution)/shard_map/while/body/eval_jaxpr/scatter-add | solution.py:76
  115.0 2.9 convert_reduce_fusion.4
  120.7 9.7 %scatter_fusion = f32[64,128,256]{2,1,0:T(8,128)} fusion(f32[64,128,256]{2,1,0:T(8,128)} %get-tuple-element.263, s32[32]{0:T(128)S(1)} %get-tuple-element.243, f32[32,128,256]{2,1,0:T(8,128)} %fusion.44), kind=kCustom, calls=%fused_computation.2.clone.1 | custom fusion | flops 1048576 | bytes 12583040 | tf_op jit(solution)/shard_map/while/body/eval_jaxpr/scatter-add | solution.py:76
  133.3 2.9 convert_reduce_fusion.4
  139.0 9.7 %scatter_fusion = f32[64,128,256]{2,1,0:T(8,128)} fusion(f32[64,128,256]{2,1,0:T(8,128)} %get-tuple-element.263, s32[32]{0:T(128)S(1)} %get-tuple-element.243, f32[32,128,256]{2,1,0:T(8,128)} %fusion.44), kind=kCustom, calls=%fused_computation.2.clone.1 | custom fusion | flops 1048576 | bytes 12583040 | tf_op jit(solution)/shard_map/while/body/eval_jaxpr/scatter-add | solution.py:76
  151.6 2.9 convert_reduce_fusion.4
  157.2 9.8 %scatter_fusion = f32[64,128,256]{2,1,0:T(8,128)} fusion(f32[64,128,256]{2,1,0:T(8,128)} %get-tuple-element.263, s32[32]{0:T(128)S(1)} %get-tuple-element.243, f32[32,128,256]{2,1,0:T(8,128)} %fusion.44), kind=kCustom, calls=%fused_computation.2.clone.1 | custom fusion | flops 1048576 | bytes 12583040 | tf_op jit(solution)/shard_map/while/body/eval_jaxpr/scatter-add | solution.py:76
  169.9 2.9 convert_reduce_fusion.4
  175.6 9.8 %scatter_fusion = f32[64,128,256]{2,1,0:T(8,128)} fusion(f32[64,128,256]{2,1,0:T(8,128)} %get-tuple-element.263, s32[32]{0:T(128)S(1)} %get-tuple-element.243, f32[32,128,256]{2,1,0:T(8,128)} %fusion.44), kind=kCustom, calls=%fused_computation.2.clone.1 | custom fusion | flops 1048576 | bytes 12583040 | tf_op jit(solution)/shard_map/while/body/eval_jaxpr/scatter-add | solution.py:76
  188.3 2.9 convert_reduce_fusion.4
  194.0 10.0 %scatter_fusion = f32[64,128,256]{2,1,0:T(8,128)} fusion(f32[64,128,256]{2,1,0:T(8,128)} %get-tuple-element.263, s32[32]{0:T(128)S(1)} %get-tuple-element.243, f32[32,128,256]{2,1,0:T(8,128)} %fusion.44), kind=kCustom, calls=%fused_computation.2.clone.1 | custom fusion | flops 1048576 | bytes 12583040 | tf_op jit(solution)/shard_map/while/body/eval_jaxpr/scatter-add | solution.py:76
  205.2 119.9 %reduce-scatter.3.cloned.1.call-done = f32[512,256]{1,0:T(8,128)} async-done(((f32[8192,256]{1,0:T(8,128)}), f32[512,256]{1,0:T(8,128)}) %reduce-scatter.3.cloned.1.call-update) | async-done | bytes 524304 | tf_op jit(solution)/shard_map/reduce_scatter | solution.py:82
  330.5 120.3 %all-reduce.7.cloned.1.call-done = (f32[256,256]{0,1:T(8,128)}, f32[256,256]{0,1:T(8,128)}) async-done(((f32[256,256]{0,1:T(8,128)}, f32[256,256]{0,1:T(8,128)}), (f32[256,256]{0,1:T(8,128)}, f32[256,256]{0,1:T(8,128)})) %all-reduce.7.cloned.1.call-update) | async-done | bytes 524304 | tf_op jit(solution)/shard_map/psum | solution.py:18
  450.9 79.2 %all-gather.5.cloned.1.call-done = bf16[8192,256]{1,0:T(8,128)(2,1)} async-done(((bf16[512,256]{1,0:T(8,128)(2,1)}), bf16[8192,256]{1,0:T(8,128)(2,1)}) %all-gather.5.cloned.1.call-update) | async-done | bytes 4194320 | tf_op jit(solution)/shard_map/all_gather | solution.py:28
  530.2 4.3 broadcast.81
  534.4 150.1 %while.21 = (s32[]{:T(128)}, f32[64,128,256]{2,1,0:T(8,128)}, s32[8,32]{1,0:T(8,128)S(1)}, s32[8,4,32,128]{3,2,1,0:T(8,128)S(1)}, f32[8,32]{1,0:T(8,128)S(1)}, /...) while((s32[]{:T(128)}, f32[64,128,256]{2,1,0:T(8,128)}, s32[8,32]{1,0:T(8,128)S(1)}, ...), condition=%wide.region_8.9_spmd, body=%wide.region_5.8_spmd.sunk | while | flops 276300992 | bytes 27465064 | solution.py:40
  537.3 2.9 convert_reduce_fusion.5
  543.2 9.9 %scatter_fusion.1 = f32[64,128,256]{2,1,0:T(8,128)} fusion(f32[64,128,256]{2,1,0:T(8,128)} %get-tuple-element.287, s32[32]{0:T(128)S(1)} %get-tuple-element.252, f32[32,128,256]{2,1,0:T(8,128)} %fusion.48), kind=kCustom, calls=%fused_computation.3.clone.1 | custom fusion | flops 1048576 | bytes 12583040 | tf_op jit(solution)/shard_map/while/body/eval_jaxpr/scatter-add | solution.py:37
  553.1 2.9 gather_fusion.1
  556.0 2.9 convert_reduce_fusion.5
  561.8 10.1 %scatter_fusion.1 = f32[64,128,256]{2,1,0:T(8,128)} fusion(f32[64,128,256]{2,1,0:T(8,128)} %get-tuple-element.287, s32[32]{0:T(128)S(1)} %get-tuple-element.252, f32[32,128,256]{2,1,0:T(8,128)} %fusion.48), kind=kCustom, calls=%fused_computation.3.clone.1 | custom fusion | flops 1048576 | bytes 12583040 | tf_op jit(solution)/shard_map/while/body/eval_jaxpr/scatter-add | solution.py:37
  571.9 2.9 gather_fusion.1
  574.8 2.9 convert_reduce_fusion.5
  580.7 10.0 %scatter_fusion.1 = f32[64,128,256]{2,1,0:T(8,128)} fusion(f32[64,128,256]{2,1,0:T(8,128)} %get-tuple-element.287, s32[32]{0:T(128)S(1)} %get-tuple-element.252, f32[32,128,256]{2,1,0:T(8,128)} %fusion.48), kind=kCustom, calls=%fused_computation.3.clone.1 | custom fusion | flops 1048576 | bytes 12583040 | tf_op jit(solution)/shard_map/while/body/eval_jaxpr/scatter-add | solution.py:37
  593.6 2.9 convert_reduce_fusion.5
  596.5 2.9 fusion.48
  599.4 10.1 %scatter_fusion.1 = f32[64,128,256]{2,1,0:T(8,128)} fusion(f32[64,128,256]{2,1,0:T(8,128)} %get-tuple-element.287, s32[32]{0:T(128)S(1)} %get-tuple-element.252, f32[32,128,256]{2,1,0:T(8,128)} %fusion.48), kind=kCustom, calls=%fused_computation.3.clone.1 | custom fusion | flops 1048576 | bytes 12583040 | tf_op jit(solution)/shard_map/while/body/eval_jaxpr/scatter-add | solution.py:37
  612.4 2.9 convert_reduce_fusion.5
  615.4 2.9 fusion.48
  618.3 10.1 %scatter_fusion.1 = f32[64,128,256]{2,1,0:T(8,128)} fusion(f32[64,128,256]{2,1,0:T(8,128)} %get-tuple-element.287, s32[32]{0:T(128)S(1)} %get-tuple-element.252, f32[32,128,256]{2,1,0:T(8,128)} %fusion.48), kind=kCustom, calls=%fused_computation.3.clone.1 | custom fusion | flops 1048576 | bytes 12583040 | tf_op jit(solution)/shard_map/while/body/eval_jaxpr/scatter-add | solution.py:37
  631.3 2.9 convert_reduce_fusion.5
  637.1 10.1 %scatter_fusion.1 = f32[64,128,256]{2,1,0:T(8,128)} fusion(f32[64,128,256]{2,1,0:T(8,128)} %get-tuple-element.287, s32[32]{0:T(128)S(1)} %get-tuple-element.252, f32[32,128,256]{2,1,0:T(8,128)} %fusion.48), kind=kCustom, calls=%fused_computation.3.clone.1 | custom fusion | flops 1048576 | bytes 12583040 | tf_op jit(solution)/shard_map/while/body/eval_jaxpr/scatter-add | solution.py:37
  650.1 2.9 convert_reduce_fusion.5
  653.0 2.9 fusion.48
  655.9 9.9 %scatter_fusion.1 = f32[64,128,256]{2,1,0:T(8,128)} fusion(f32[64,128,256]{2,1,0:T(8,128)} %get-tuple-element.287, s32[32]{0:T(128)S(1)} %get-tuple-element.252, f32[32,128,256]{2,1,0:T(8,128)} %fusion.48), kind=kCustom, calls=%fused_computation.3.clone.1 | custom fusion | flops 1048576 | bytes 12583040 | tf_op jit(solution)/shard_map/while/body/eval_jaxpr/scatter-add | solution.py:37
  668.7 2.9 convert_reduce_fusion.5
  671.7 2.9 fusion.48
  674.6 9.9 %scatter_fusion.1 = f32[64,128,256]{2,1,0:T(8,128)} fusion(f32[64,128,256]{2,1,0:T(8,128)} %get-tuple-element.287, s32[32]{0:T(128)S(1)} %get-tuple-element.252, f32[32,128,256]{2,1,0:T(8,128)} %fusion.48), kind=kCustom, calls=%fused_computation.3.clone.1 | custom fusion | flops 1048576 | bytes 12583040 | tf_op jit(solution)/shard_map/while/body/eval_jaxpr/scatter-add | solution.py:37
  684.5 13.9 %all-reduce.5.cloned.1.call-done = (f32[256,256]{0,1:T(8,128)}, f32[256,256]{0,1:T(8,128)}) async-done(((f32[256,256]{0,1:T(8,128)}, f32[256,256]{0,1:T(8,128)}), (f32[256,256]{0,1:T(8,128)}, f32[256,256]{0,1:T(8,128)})) %all-reduce.5.cloned.1.call-update) | async-done | bytes 524304 | tf_op jit(solution)/shard_map/psum | solution.py:19
  701.2 99.0 %reduce-scatter.5.cloned.1.call-done = f32[512,256]{1,0:T(8,128)} async-done(((f32[8192,256]{1,0:T(8,128)}), f32[512,256]{1,0:T(8,128)}) %reduce-scatter.5.cloned.1.call-update) | async-done | bytes 524304 | tf_op jit(solution)/shard_map/reduce_scatter | solution.py:43
  (127 shorter events, 88.7 us)
Async XLA Ops:
  7.2 319.2 %copy-start = (bf16[256,256]{1,0:T(8,128)(2,1)S(1)}, bf16[256,256]{1,0:T(8,128)(2,1)}, u32[]{:S(2)}) copy-start(bf16[256,256]{1,0:T(8,128)(2,1)} %param.15) | copy-start | bytes 393220
  7.2 45.7 %all-gather.3.cloned.1.call-start = ((), (), s32[]{:S(2)}) async-start(), calls=%async_computation.2 | async-start | bytes 4456448 | tf_op jit(solution)/shard_map/all_gather | solution.py:67
  7.9 317.2 %reduce-scatter.3.cloned.1.call-start = ((), (), s32[]{:S(2)}) async-start(), calls=%async_computation.3 | async-start | bytes 8912896 | tf_op jit(solution)/shard_map/reduce_scatter | solution.py:82
  204.0 0.7 copy-start.3
  204.0 1.0 copy-start.1
  204.0 1.0 copy-start.2
  204.0 122.4 %copy-start.4 = (bf16[512,256]{1,0:T(8,128)(2,1)S(1)}, bf16[512,256]{1,0:T(8,128)(2,1)}, u32[]{:S(2)}) copy-start(bf16[512,256]{1,0:T(8,128)(2,1)} %param.16) | copy-start | bytes 786436
  204.0 246.8 %all-reduce.7.cloned.1.call-start = ((), (), s32[]{:S(2)}) async-start(), calls=%async_computation.7 | async-start | bytes 1048576 | tf_op jit(solution)/shard_map/psum | solution.py:18
  329.4 200.7 %all-gather.5.cloned.1.call-start = ((), (), s32[]{:S(2)}) async-start(), calls=%async_computation.4 | async-start | bytes 4456448 | tf_op jit(solution)/shard_map/all_gather | solution.py:28
  330.5 367.9 %all-reduce.5.cloned.1.call-start = ((), (), s32[]{:S(2)}) async-start(), calls=%async_computation.6 | async-start | bytes 1048576 | tf_op jit(solution)/shard_map/psum | solution.py:19
  450.9 349.3 %reduce-scatter.5.cloned.1.call-start = ((), (), s32[]{:S(2)}) async-start(), calls=%async_computation.5 | async-start | bytes 8912896 | tf_op jit(solution)/shard_map/reduce_scatter | solution.py:43
Sparse Core Ops, SparseCore 0:
  9.9 42.9 all-gather.2
  204.1 120.9 reduce-scatter.2
  329.6 121.2 all-reduce.6
  454.0 76.1 all-gather.4
  532.9 165.5 all-reduce.4
  700.8 99.2 reduce-scatter.4
